TPU v7x, 32 devices: a whole 2x2x4 slice. The times are simulated.
32 devices in a mesh: row: 8 (over z, x), col: 4 (over y, core).
Axes of the slice: x: 2, y: 2, z: 4, core: 2. Of those that a mesh axis runs over, the one named last changes fastest.
Arguments:
- tokens: bfloat16 [2, 8192, 768], P(None, ('row', 'col')), may hold values from -6 to 6
- segments: int32 [2, 8192], P(None, ('row', 'col')), may hold values from 0 to 17, as said below
- positions: int32 [2, 8192], P(None, ('row', 'col')), may hold values from 0 to 799, as said below
- w_qkv: bfloat16 [768, 3, 768], P('row', None, 'col'), may hold values from -0.21875 to 0.21875
- w_out: bfloat16 [768, 768], P('col', 'row'), may hold values from -0.875 to 0.875
- w_gate_up: bfloat16 [768, 2, 3072], P('row', None, 'col'), may hold values from -0.21875 to 0.21875
- w_down: bfloat16 [3072, 768], P('col', 'row'), may hold values from -0.109375 to 0.109375
- norm_gain: bfloat16 [768, 2], P('row'), may hold values from 0.5 to 1.5
- norm_bias: bfloat16 [768, 2], P('row'), may hold values from -1.1953125 to 1.1953125
- cotangent: float32 [2, 8192, 768], P(None, ('row', 'col')), may hold values from -6 to 6
Outputs:
- layer_out: bfloat16 [2, 8192, 768], P(None, ('row', 'col'))
- input_grad: float32 [2, 8192, 768], P(None, ('row', 'col'))
- grad_qkv: float32 [768, 3, 768], P('row', None, 'col')
- grad_out: float32 [768, 768], P('col', 'row')
- grad_gate_up: float32 [768, 2, 3072], P('row', None, 'col')
- grad_down: float32 [3072, 768], P('col', 'row')
- grad_gain: float32 [768, 2], P('row')
- grad_bias: float32 [768, 2], P('row')
Inputs may be any that keep to these rules, and one draw needn't show every extreme that they name: `segments`: within each sequence documents are numbered from 0 upward and never fall; a document has at most 800 tokens and at least 60 unless it is the last of its sequence; some document has exactly 800 tokens, and in some sequence every document but the last has exactly 60 tokens. `positions`: the place of each token within its document, counted from 0.
All inputs are finite; a program needn't handle non-finite values.
Results may differ from a plain program's by a relative error of at most 0.017.
Values may be sent and summed in bfloat16 or wider, within the bound.
No kernel may reach another device: no remote copies, remote signals or barrier semaphores. Data moves between devices by JAX's collectives and lax.ppermute only.
A program may use at most 192 MiB of HBM per device.

v0:
```python
import math
import jax
import jax.numpy as jnp
from jax import lax
from jax.sharding import PartitionSpec as P

HD = 64
LEN = 1024
epsilon = 1e-12
rope_base = 1000.0
masked_score = -1e30


def in_blocks(array, dim, peers):
    dims = array.shape
    blocks = array.reshape(*dims[:dim], peers, dims[dim] // peers, *dims[dim + 1 :])
    return jnp.moveaxis(blocks, dim, 0)


def summed_on_arrival(array, axis, dim):
    blocks = in_blocks(array, dim, lax.axis_size(axis))
    arrived = lax.all_to_all(blocks, axis, split_axis=0, concat_axis=0, tiled=True)
    return arrived.astype(jnp.float32).sum(axis=0)


def sent_together(arrays, axis, dim, along):
    widths = [math.prod(a.shape[along:]) for a in arrays]
    both = jnp.concatenate(
        [a.reshape(*a.shape[:along], w) for a, w in zip(arrays, widths)], axis=along
    )
    out = summed_on_arrival(both, axis, dim)
    blocks = jnp.split(out, [sum(widths[:k]) for k in range(1, len(widths))], axis=along)
    return tuple((b.reshape(*out.shape[:along], *a.shape[along:]) for a, b in zip(arrays, blocks)))


def sent_together_2(arrays, axis, dim, along):
    widths = [a.shape[along] for a in arrays]
    both = jnp.concatenate(arrays, axis=along)
    out = summed_on_arrival(both, axis, dim)
    return tuple(jnp.split(out, [sum(widths[:k]) for k in range(1, len(widths))], axis=along))


def rope_tables(positions):
    half_dim = HD // 2
    freq = rope_base ** (-jnp.arange(half_dim, dtype=jnp.float32) / half_dim)
    angles = positions.astype(jnp.float32)[:, None] * freq[None, :]
    return (jnp.cos(angles), jnp.sin(angles))


def rotate(values, cosine, sine):
    half_dim = HD // 2
    first = values[..., :half_dim]
    second = values[..., half_dim:]
    cosine = cosine[:, None, :]
    sine = sine[:, None, :]
    return jnp.concatenate(
        [first * cosine - second * sine, second * cosine + first * sine], axis=-1
    )


def unrotate(grad_vals, cosine, sine):
    half_dim = HD // 2
    first = grad_vals[..., :half_dim]
    second = grad_vals[..., half_dim:]
    cosine = cosine[:, None, :]
    sine = sine[:, None, :]
    return jnp.concatenate(
        [first * cosine + second * sine, second * cosine - first * sine], axis=-1
    )


def normalize(hidden):
    centred = hidden - jnp.mean(hidden, axis=-1, keepdims=True)
    variance = jnp.mean(centred * centred, axis=-1, keepdims=True)
    inv_std = lax.rsqrt(variance + epsilon)
    return (centred * inv_std, inv_std)


def norm_back(grad_norm, normed, inv_std):
    return inv_std * (
        grad_norm
        - jnp.mean(grad_norm, axis=-1, keepdims=True)
        - normed * jnp.mean(grad_norm * normed, axis=-1, keepdims=True)
    )


def gather_tokens(values):
    return lax.all_gather(values, "col", axis=0, tiled=True)


def token_sums(left, right, contract):
    row_count = left.shape[0] // lax.axis_size("col")
    piece = lax.slice_in_dim(left, 0, lax.axis_size("col") * row_count, axis=0)
    return lax.psum_scatter(
        lax.dot_general(
            piece, right, (((1,), (contract,)), ((), ())), preferred_element_type=jnp.float32
        ).astype(jnp.bfloat16),
        "col",
        scatter_dimension=0,
        tiled=True,
    ).astype(jnp.float32)


def fetch_weights(w_qkv, w_out, w_gate_up, w_down, norm_gain, norm_bias):
    qkv_full, gate_up_full, gain_full, bias_full = (
        lax.all_gather(w_qkv, "row", axis=0, tiled=True),
        lax.all_gather(w_gate_up, "row", axis=0, tiled=True),
        lax.all_gather(norm_gain, "row", axis=0, tiled=True),
        lax.all_gather(norm_bias, "row", axis=0, tiled=True),
    )
    out_full, down_full = (
        lax.all_gather(w_out, "row", axis=1, tiled=True),
        lax.all_gather(w_down, "row", axis=1, tiled=True),
    )
    width = qkv_full.shape[0]
    return (
        qkv_full.reshape(width, -1),
        out_full,
        gate_up_full.reshape(width, -1),
        down_full,
        gain_full.astype(jnp.float32),
        bias_full.astype(jnp.float32),
    )


def key_window(seq_len, low_row):
    span = min(LEN, seq_len)
    return (low_row // span * span, span)


def attend(queries, keys, values, segment):
    seq_len = queries.shape[0]
    block_rows = min(512, LEN, seq_len)
    scale = 1.0 / math.sqrt(HD)
    outs_list = []
    totals_list = []
    for block_number in range(seq_len // block_rows):
        low_row = block_number * block_rows
        key_start, span = key_window(seq_len, low_row)
        rows_q = queries[low_row : low_row + block_rows]
        scores = (
            jnp.einsum("qhd,khd->hqk", rows_q, keys, preferred_element_type=jnp.float32) * scale
        )
        same_doc = (
            segment[low_row : low_row + block_rows, None]
            == segment[None, key_start : key_start + span]
        )
        scores = jnp.where(same_doc[None], scores, masked_score)
        row_max = jnp.max(scores, axis=-1, keepdims=True)
        expo = jnp.exp(scores - row_max)
        row_sum = jnp.sum(expo, axis=-1, keepdims=True)
        probs = (expo / row_sum).astype(jnp.bfloat16)
        outs_list.append(
            jnp.einsum("hqk,khd->qhd", probs, values, preferred_element_type=jnp.float32).astype(
                jnp.bfloat16
            )
        )
        totals_list.append(row_max + jnp.log(row_sum))
    return (jnp.concatenate(outs_list, axis=0), jnp.concatenate(totals_list, axis=1))


def attend_back(queries, keys, values, log_total, grad_att, segment):
    seq_len = queries.shape[0]
    block_rows = min(512, LEN, seq_len)
    scale = 1.0 / math.sqrt(HD)
    grad_q_list = []
    grad_k = jnp.zeros(keys.shape, jnp.float32)
    grad_v = jnp.zeros(values.shape, jnp.float32)
    for block_number in range(seq_len // block_rows):
        low_row = block_number * block_rows
        key_start, span = key_window(seq_len, low_row)
        rows_q = queries[low_row : low_row + block_rows]
        rows_grad = grad_att[low_row : low_row + block_rows]
        keys_seq = keys[key_start : key_start + span]
        values_seq = values[key_start : key_start + span]
        scores = (
            jnp.einsum("qhd,khd->hqk", rows_q, keys_seq, preferred_element_type=jnp.float32) * scale
        )
        same_doc = (
            segment[low_row : low_row + block_rows, None]
            == segment[None, key_start : key_start + span]
        )
        scores = jnp.where(same_doc[None], scores, masked_score)
        probs = jnp.exp(scores - log_total[:, low_row : low_row + block_rows])
        probs_low = probs.astype(jnp.bfloat16)
        grad_probs = jnp.einsum(
            "qhd,khd->hqk", rows_grad, values_seq, preferred_element_type=jnp.float32
        )
        delta_sum = jnp.sum(probs * grad_probs, axis=-1, keepdims=True)
        grad_scores = (probs * (grad_probs - delta_sum)).astype(jnp.bfloat16)
        grad_q_list.append(
            jnp.einsum("hqk,khd->qhd", grad_scores, keys_seq, preferred_element_type=jnp.float32)
            * scale
        )
        grad_k = grad_k.at[key_start : key_start + span].add(
            jnp.einsum("hqk,qhd->khd", grad_scores, rows_q, preferred_element_type=jnp.float32)
            * scale
        )
        grad_v = grad_v.at[key_start : key_start + span].add(
            jnp.einsum("hqk,qhd->khd", probs_low, rows_grad, preferred_element_type=jnp.float32)
        )
    return (jnp.concatenate(grad_q_list, axis=0), grad_k, grad_v)


def on_device(
    tokens, segments, positions, w_qkv, w_out, w_gate_up, w_down, norm_gain, norm_bias, cotangent
):
    doc_ids, doc_places = (
        lax.all_gather(segments, "col", axis=1, tiled=True),
        lax.all_gather(positions, "col", axis=1, tiled=True),
    )

    def current_weights():
        return fetch_weights(w_qkv, w_out, w_gate_up, w_down, norm_gain, norm_bias)

    def forward_step(carry, items):
        inputs, segment, place = items
        qkv_w, out_w, gate_up_w, down_w, gains, biases = current_weights()
        seq_inputs = gather_tokens(inputs)
        seq_len = seq_inputs.shape[0]
        proj = jnp.dot(seq_inputs, qkv_w, preferred_element_type=jnp.float32).reshape(
            seq_len, 3, -1, HD
        )
        cosine, sine = rope_tables(place)
        queries = rotate(proj[:, 0], cosine, sine).astype(jnp.bfloat16)
        keys = rotate(proj[:, 1], cosine, sine).astype(jnp.bfloat16)
        values = proj[:, 2].astype(jnp.bfloat16)
        attended, log_total = attend(queries, keys, values, segment)
        flat_attended = attended.reshape(seq_len, -1)
        branch = token_sums(flat_attended, out_w, 0)
        first_normed, first_inv = normalize(inputs.astype(jnp.float32) + branch)
        first_out = first_normed * gains[:, 0] + biases[:, 0]
        seq_normed = gather_tokens(first_out.astype(jnp.bfloat16))
        gate_up = jnp.dot(seq_normed, gate_up_w, preferred_element_type=jnp.float32)
        half_cols = gate_up.shape[1] // 2
        hidden = (jax.nn.silu(gate_up[:, :half_cols]) * gate_up[:, half_cols:]).astype(jnp.bfloat16)
        feed = token_sums(hidden, down_w, 0)
        second_normed, second_inv = normalize(first_out + feed)
        outputs = (second_normed * gains[:, 1] + biases[:, 1]).astype(jnp.bfloat16)
        kept = (
            seq_inputs,
            queries,
            keys,
            values,
            flat_attended,
            log_total,
            seq_normed,
            gate_up,
            first_normed,
            first_inv,
            second_normed,
            second_inv,
        )
        return (carry, (outputs, kept))

    unused, (layer_out, kept_all) = lax.scan(
        forward_step, jnp.zeros((), jnp.float32), (tokens, doc_ids, doc_places)
    )

    def backward_step(totals, items):
        grad_y, segment, place, kept = items
        (
            seq_inputs,
            queries,
            keys,
            values,
            flat_attended,
            log_total,
            seq_normed,
            gate_up,
            first_normed,
            first_inv,
            second_normed,
            second_inv,
        ) = kept
        total_qkv, total_out, total_gate_up, total_down, total_gain, total_bias = totals
        qkv_w, out_w, gate_up_w, down_w, gains, biases = current_weights()
        seq_len = seq_inputs.shape[0]
        gain_two = jnp.sum(grad_y * second_normed, axis=0)
        bias_two = jnp.sum(grad_y, axis=0)
        grad_h2 = norm_back(grad_y * gains[:, 1], second_normed, second_inv)
        seq_grad_feed = gather_tokens(grad_h2.astype(jnp.bfloat16))
        grad_hidden = lax.dot_general(
            seq_grad_feed, down_w, (((1,), (1,)), ((), ())), preferred_element_type=jnp.float32
        )
        half_cols = gate_up.shape[1] // 2
        gate = gate_up[:, :half_cols]
        up_part = gate_up[:, half_cols:]
        sigma = jax.nn.sigmoid(gate)
        silu_gate = gate * sigma
        grad_gate = grad_hidden * up_part * sigma * (1.0 + gate * (1.0 - sigma))
        grad_up = grad_hidden * silu_gate
        grad_gate_up = jnp.concatenate([grad_gate, grad_up], axis=1).astype(jnp.bfloat16)
        hidden = (silu_gate * up_part).astype(jnp.bfloat16)
        total_down = total_down + lax.dot_general(
            hidden, seq_grad_feed, (((0,), (0,)), ((), ())), preferred_element_type=jnp.float32
        )
        total_gate_up = total_gate_up + lax.dot_general(
            seq_normed, grad_gate_up, (((0,), (0,)), ((), ())), preferred_element_type=jnp.float32
        )
        grad_first = grad_h2 + token_sums(grad_gate_up, gate_up_w, 1)
        gain_one = jnp.sum(grad_first * first_normed, axis=0)
        bias_one = jnp.sum(grad_first, axis=0)
        grad_h1 = norm_back(grad_first * gains[:, 0], first_normed, first_inv)
        seq_grad_branch = gather_tokens(grad_h1.astype(jnp.bfloat16))
        total_out = total_out + lax.dot_general(
            flat_attended,
            seq_grad_branch,
            (((0,), (0,)), ((), ())),
            preferred_element_type=jnp.float32,
        )
        grad_att = lax.dot_general(
            seq_grad_branch, out_w, (((1,), (1,)), ((), ())), preferred_element_type=jnp.float32
        )
        grad_att = grad_att.astype(jnp.bfloat16).reshape(seq_len, -1, HD)
        grad_q, grad_k, grad_v = attend_back(queries, keys, values, log_total, grad_att, segment)
        cosine, sine = rope_tables(place)
        grad_proj = jnp.stack(
            [unrotate(grad_q, cosine, sine), unrotate(grad_k, cosine, sine), grad_v], axis=1
        )
        grad_proj = grad_proj.reshape(seq_len, -1).astype(jnp.bfloat16)
        total_qkv = total_qkv + lax.dot_general(
            seq_inputs, grad_proj, (((0,), (0,)), ((), ())), preferred_element_type=jnp.float32
        )
        grad_inputs = grad_h1 + token_sums(grad_proj, qkv_w, 1)
        total_gain = total_gain + jnp.stack([gain_one, gain_two], axis=1)
        total_bias = total_bias + jnp.stack([bias_one, bias_two], axis=1)
        return (
            (total_qkv, total_out, total_gate_up, total_down, total_gain, total_bias),
            grad_inputs,
        )

    width = tokens.shape[2]
    head_cols = w_qkv.shape[2]
    hidden_cols = w_gate_up.shape[2]
    zero_sums = (
        jnp.zeros((width, 3 * head_cols), jnp.float32),
        jnp.zeros((head_cols, width), jnp.float32),
        jnp.zeros((width, 2 * hidden_cols), jnp.float32),
        jnp.zeros((hidden_cols, width), jnp.float32),
        jnp.zeros((width, 2), jnp.float32),
        jnp.zeros((width, 2), jnp.float32),
    )
    totals, input_grad = lax.scan(
        backward_step, zero_sums, (cotangent, doc_ids, doc_places, kept_all)
    )
    total_qkv = totals[0].reshape(width, 3, head_cols)
    total_gate_up = totals[2].reshape(width, 2, hidden_cols)
    grad_qkv, grad_gate_up, grad_gain, grad_bias = sent_together(
        (
            total_qkv.astype(jnp.bfloat16),
            total_gate_up.astype(jnp.bfloat16),
            totals[4].astype(jnp.bfloat16),
            totals[5].astype(jnp.bfloat16),
        ),
        "row",
        0,
        1,
    )
    grad_out, grad_down = sent_together_2(
        (totals[1].astype(jnp.bfloat16), totals[3].astype(jnp.bfloat16)), "row", 1, 0
    )
    grad_gain, grad_bias = lax.psum((grad_gain, grad_bias), "col")
    return (
        layer_out,
        input_grad,
        grad_qkv,
        grad_out,
        grad_gate_up,
        grad_down,
        grad_gain,
        grad_bias,
    )


def solution(mesh):
    in_specs = (
        P(None, ("row", "col"), None),
        P(None, ("row", "col")),
        P(None, ("row", "col")),
        P("row", None, "col"),
        P("col", "row"),
        P("row", None, "col"),
        P("col", "row"),
        P("row", None),
        P("row", None),
        P(None, ("row", "col"), None),
    )
    out_specs = (
        P(None, ("row", "col"), None),
        P(None, ("row", "col"), None),
        P("row", None, "col"),
        P("col", "row"),
        P("row", None, "col"),
        P("col", "row"),
        P("row", None),
        P("row", None),
    )
    return jax.shard_map(
        on_device, mesh=mesh, in_specs=in_specs, out_specs=out_specs, check_vma=False
    )
```

profile of v0, /device:TPU:0, one launch (start us, length us, event | category | flops | bytes accessed | tf_op | source)
XLA Modules:
  0.0 1322.1 jit_solution(584793681520028164)
XLA Ops:
  25.1 542.4 %while.68 = (s32[]{:T(128)}, bf16[2,256,768]{2,1,0:T(8,128)(2,1)}, bf16[2,1024,768]{2,1,0:T(8,128)(2,1)}, bf16[2,1024,3,64]{1,3,2,0:T(8,128)(2,1)}, bf16[2,1024,...) while((s32[]{:T(128)}, bf16[2,256,768]{2,1,0:T(8,128)(2,1)}, ...), condition=%wide.region_11.12_spmd, body=%wide.region_0.11_spmd.sunk | while | flops 5697212928 | bytes 190405408 | solution.py:256
  26.1 37.9 %all_gather.99 = bf16[768,3,192]{2,1,0:T(4,128)(2,1)S(1)} all-gather(bf16[96,3,192]{2,1,0:T(4,128)(2,1)S(1)} %get-tuple-element.1742), channel_id=1, replica_groups=mesh['row'=8,'col'=4] {'row'}, dimensions={0}, use_global_device_ids=true | all-gather | bytes 995328 | tf_op jit(solution)/shard_map/while/body/eval_jaxpr/all_gather | solution.py:106
  66.8 31.1 %all_gather.100 = bf16[192,768]{0,1:T(8,128)(2,1)S(1)} all-gather(bf16[192,96]{0,1:T(8,128)(2,1)S(1)} %get-tuple-element.1745), channel_id=1, replica_groups=mesh['row'=8,'col'=4] {'row'}, dimensions={1}, use_global_device_ids=true | all-gather | bytes 331776 | tf_op jit(solution)/shard_map/while/body/eval_jaxpr/all_gather | solution.py:112
  115.7 18.5 %all-gather.11 = bf16[8,96,2]{1,2,0:T(2,128)(2,1)S(1)} all-gather(bf16[1,96,2]{1,2,0:T(2,128)(2,1)} %bitcast.350), channel_id=1, replica_groups=mesh['row'=8,'col'=4] {'row'}, dimensions={0}, use_global_device_ids=true | all-gather | bytes 3456 | tf_op jit(solution)/shard_map/while/body/eval_jaxpr/all_gather | solution.py:108
  134.3 16.4 %all-gather.10 = bf16[8,96,2]{1,2,0:T(2,128)(2,1)S(1)} all-gather(bf16[1,96,2]{1,2,0:T(2,128)(2,1)} %bitcast.349), channel_id=1, replica_groups=mesh['row'=8,'col'=4] {'row'}, dimensions={0}, use_global_device_ids=true | all-gather | bytes 3456 | tf_op jit(solution)/shard_map/while/body/eval_jaxpr/all_gather | solution.py:109
  157.1 38.9 %all-gather.28.cloned.1.call-done = bf16[768,2,768]{2,1,0:T(2,128)(2,1)} async-done(((bf16[96,2,768]{2,1,0:T(2,128)(2,1)}), bf16[768,2,768]{2,1,0:T(2,128)(2,1)}) %all-gather.28.cloned.1.call-update) | async-done | bytes 2359312 | tf_op jit(solution)/shard_map/while/body/eval_jaxpr/all_gather | solution.py:107
  198.1 18.2 %all-gather.26.cloned.1.call-done = bf16[1024,768]{1,0:T(8,128)(2,1)} async-done(((bf16[256,768]{1,0:T(8,128)(2,1)}), bf16[1024,768]{1,0:T(8,128)(2,1)}) %all-gather.26.cloned.1.call-update) | async-done | bytes 1572880 | tf_op jit(solution)/shard_map/while/body/eval_jaxpr/all_gather | solution.py:88
  223.8 35.6 %all-gather.22.cloned.1.call-done = bf16[768,768]{0,1:T(8,128)(2,1)} async-done(((bf16[768,96]{0,1:T(8,128)(2,1)}), bf16[768,768]{0,1:T(8,128)(2,1)}) %all-gather.22.cloned.1.call-update) | async-done | bytes 1179664 | tf_op jit(solution)/shard_map/while/body/eval_jaxpr/all_gather | solution.py:113
  276.4 16.5 %reduce-scatter.7.cloned.1.call-done = bf16[256,768]{1,0:T(8,128)(2,1)} async-done(((bf16[1024,768]{1,0:T(8,128)(2,1)}), bf16[256,768]{1,0:T(8,128)(2,1)}) %reduce-scatter.7.cloned.1.call-update) | async-done | bytes 393232 | tf_op jit(solution)/shard_map/while/body/eval_jaxpr/reduce_scatter | solution.py:94
  297.7 37.2 %all_gather.99 = bf16[768,3,192]{2,1,0:T(4,128)(2,1)S(1)} all-gather(bf16[96,3,192]{2,1,0:T(4,128)(2,1)S(1)} %get-tuple-element.1742), channel_id=1, replica_groups=mesh['row'=8,'col'=4] {'row'}, dimensions={0}, use_global_device_ids=true | all-gather | bytes 995328 | tf_op jit(solution)/shard_map/while/body/eval_jaxpr/all_gather | solution.py:106
  337.7 31.2 %all_gather.100 = bf16[192,768]{0,1:T(8,128)(2,1)S(1)} all-gather(bf16[192,96]{0,1:T(8,128)(2,1)S(1)} %get-tuple-element.1745), channel_id=1, replica_groups=mesh['row'=8,'col'=4] {'row'}, dimensions={1}, use_global_device_ids=true | all-gather | bytes 331776 | tf_op jit(solution)/shard_map/while/body/eval_jaxpr/all_gather | solution.py:112
  386.7 18.3 %all-gather.11 = bf16[8,96,2]{1,2,0:T(2,128)(2,1)S(1)} all-gather(bf16[1,96,2]{1,2,0:T(2,128)(2,1)} %bitcast.350), channel_id=1, replica_groups=mesh['row'=8,'col'=4] {'row'}, dimensions={0}, use_global_device_ids=true | all-gather | bytes 3456 | tf_op jit(solution)/shard_map/while/body/eval_jaxpr/all_gather | solution.py:108
  405.1 16.4 %all-gather.10 = bf16[8,96,2]{1,2,0:T(2,128)(2,1)S(1)} all-gather(bf16[1,96,2]{1,2,0:T(2,128)(2,1)} %bitcast.349), channel_id=1, replica_groups=mesh['row'=8,'col'=4] {'row'}, dimensions={0}, use_global_device_ids=true | all-gather | bytes 3456 | tf_op jit(solution)/shard_map/while/body/eval_jaxpr/all_gather | solution.py:109
  428.0 38.5 %all-gather.28.cloned.1.call-done = bf16[768,2,768]{2,1,0:T(2,128)(2,1)} async-done(((bf16[96,2,768]{2,1,0:T(2,128)(2,1)}), bf16[768,2,768]{2,1,0:T(2,128)(2,1)}) %all-gather.28.cloned.1.call-update) | async-done | bytes 2359312 | tf_op jit(solution)/shard_map/while/body/eval_jaxpr/all_gather | solution.py:107
  468.7 18.2 %all-gather.26.cloned.1.call-done = bf16[1024,768]{1,0:T(8,128)(2,1)} async-done(((bf16[256,768]{1,0:T(8,128)(2,1)}), bf16[1024,768]{1,0:T(8,128)(2,1)}) %all-gather.26.cloned.1.call-update) | async-done | bytes 1572880 | tf_op jit(solution)/shard_map/while/body/eval_jaxpr/all_gather | solution.py:88
  494.4 35.7 %all-gather.22.cloned.1.call-done = bf16[768,768]{0,1:T(8,128)(2,1)} async-done(((bf16[768,96]{0,1:T(8,128)(2,1)}), bf16[768,768]{0,1:T(8,128)(2,1)}) %all-gather.22.cloned.1.call-update) | async-done | bytes 1179664 | tf_op jit(solution)/shard_map/while/body/eval_jaxpr/all_gather | solution.py:113
  547.1 16.5 %reduce-scatter.7.cloned.1.call-done = bf16[256,768]{1,0:T(8,128)(2,1)} async-done(((bf16[1024,768]{1,0:T(8,128)(2,1)}), bf16[256,768]{1,0:T(8,128)(2,1)}) %reduce-scatter.7.cloned.1.call-update) | async-done | bytes 393232 | tf_op jit(solution)/shard_map/while/body/eval_jaxpr/reduce_scatter | solution.py:94
  568.7 603.9 %while.69 = (s32[]{:T(128)}, f32[768,576]{0,1:T(8,128)}, f32[192,768]{1,0:T(8,128)}, f32[768,1536]{1,0:T(8,128)}, f32[768,768]{1,0:T(8,128)}, /*index=5*/f32[768...) while((s32[]{:T(128)}, f32[768,576]{0,1:T(8,128)}, ...), condition=%wide.region_25.26_spmd.clone, body=%wide.region_12.25_spmd.clone.sunk | while | flops 11771122688 | bytes 393030208 | solution.py:344
  589.5 20.5 %all-gather.12 = bf16[8,96,2]{1,2,0:T(2,128)(2,1)S(1)} all-gather(bf16[1,96,2]{1,2,0:T(2,128)(2,1)} %bitcast.403), channel_id=1, replica_groups=mesh['row'=8,'col'=4] {'row'}, dimensions={0}, use_global_device_ids=true | all-gather | bytes 3456 | tf_op jit(solution)/shard_map/while/body/eval_jaxpr/all_gather | solution.py:108
  632.8 19.9 %all-gather.32.cloned.1.call-done = bf16[1024,768]{1,0:T(8,128)(2,1)} async-done(((bf16[256,768]{1,0:T(8,128)(2,1)}), bf16[1024,768]{1,0:T(8,128)(2,1)}) %all-gather.32.cloned.1.call-update) | async-done | bytes 1572880 | tf_op jit(solution)/shard_map/while/body/eval_jaxpr/all_gather | solution.py:88
  660.5 46.3 %all-gather.30.cloned.1.call-done = bf16[768,2,768]{2,1,0:T(2,128)(2,1)} async-done(((bf16[96,2,768]{2,1,0:T(2,128)(2,1)}), bf16[768,2,768]{2,1,0:T(2,128)(2,1)}) %all-gather.30.cloned.1.call-update) | async-done | bytes 2359312 | tf_op jit(solution)/shard_map/while/body/eval_jaxpr/all_gather | solution.py:107
  713.3 26.8 %reduce-scatter.9.cloned.1.call-done = bf16[256,768]{1,0:T(8,128)(2,1)} async-done(((bf16[1024,768]{1,0:T(8,128)(2,1)}), bf16[256,768]{1,0:T(8,128)(2,1)}) %reduce-scatter.9.cloned.1.call-update) | async-done | bytes 393232 | tf_op jit(solution)/shard_map/while/body/eval_jaxpr/reduce_scatter | solution.py:94
  744.3 37.3 %all_gather.108 = bf16[768,3,192]{2,1,0:T(4,128)(2,1)S(1)} all-gather(bf16[96,3,192]{2,1,0:T(4,128)(2,1)S(1)} %get-tuple-element.1842), channel_id=1, replica_groups=mesh['row'=8,'col'=4] {'row'}, dimensions={0}, use_global_device_ids=true | all-gather | bytes 995328 | tf_op jit(solution)/shard_map/while/body/eval_jaxpr/all_gather | solution.py:106
  784.5 31.0 %all_gather.107 = bf16[192,768]{0,1:T(8,128)(2,1)S(1)} all-gather(bf16[192,96]{0,1:T(8,128)(2,1)S(1)} %get-tuple-element.1837), channel_id=1, replica_groups=mesh['row'=8,'col'=4] {'row'}, dimensions={1}, use_global_device_ids=true | all-gather | bytes 331776 | tf_op jit(solution)/shard_map/while/body/eval_jaxpr/all_gather | solution.py:112
  880.8 20.6 %all-gather.12 = bf16[8,96,2]{1,2,0:T(2,128)(2,1)S(1)} all-gather(bf16[1,96,2]{1,2,0:T(2,128)(2,1)} %bitcast.403), channel_id=1, replica_groups=mesh['row'=8,'col'=4] {'row'}, dimensions={0}, use_global_device_ids=true | all-gather | bytes 3456 | tf_op jit(solution)/shard_map/while/body/eval_jaxpr/all_gather | solution.py:108
  924.1 19.9 %all-gather.32.cloned.1.call-done = bf16[1024,768]{1,0:T(8,128)(2,1)} async-done(((bf16[256,768]{1,0:T(8,128)(2,1)}), bf16[1024,768]{1,0:T(8,128)(2,1)}) %all-gather.32.cloned.1.call-update) | async-done | bytes 1572880 | tf_op jit(solution)/shard_map/while/body/eval_jaxpr/all_gather | solution.py:88
  951.8 46.5 %all-gather.30.cloned.1.call-done = bf16[768,2,768]{2,1,0:T(2,128)(2,1)} async-done(((bf16[96,2,768]{2,1,0:T(2,128)(2,1)}), bf16[768,2,768]{2,1,0:T(2,128)(2,1)}) %all-gather.30.cloned.1.call-update) | async-done | bytes 2359312 | tf_op jit(solution)/shard_map/while/body/eval_jaxpr/all_gather | solution.py:107
  1004.8 26.8 %reduce-scatter.9.cloned.1.call-done = bf16[256,768]{1,0:T(8,128)(2,1)} async-done(((bf16[1024,768]{1,0:T(8,128)(2,1)}), bf16[256,768]{1,0:T(8,128)(2,1)}) %reduce-scatter.9.cloned.1.call-update) | async-done | bytes 393232 | tf_op jit(solution)/shard_map/while/body/eval_jaxpr/reduce_scatter | solution.py:94
  1035.7 37.0 %all_gather.108 = bf16[768,3,192]{2,1,0:T(4,128)(2,1)S(1)} all-gather(bf16[96,3,192]{2,1,0:T(4,128)(2,1)S(1)} %get-tuple-element.1842), channel_id=1, replica_groups=mesh['row'=8,'col'=4] {'row'}, dimensions={0}, use_global_device_ids=true | all-gather | bytes 995328 | tf_op jit(solution)/shard_map/while/body/eval_jaxpr/all_gather | solution.py:106
  1075.6 31.2 %all_gather.107 = bf16[192,768]{0,1:T(8,128)(2,1)S(1)} all-gather(bf16[192,96]{0,1:T(8,128)(2,1)S(1)} %get-tuple-element.1837), channel_id=1, replica_groups=mesh['row'=8,'col'=4] {'row'}, dimensions={1}, use_global_device_ids=true | all-gather | bytes 331776 | tf_op jit(solution)/shard_map/while/body/eval_jaxpr/all_gather | solution.py:112
  1194.5 25.8 %all-to-all-done.1 = bf16[8,960,96]{1,2,0:T(8,128)(2,1)} async-done(((bf16[8,960,96]{1,2,0:T(8,128)(2,1)}), bf16[8,960,96]{1,2,0:T(8,128)(2,1)}, u32[]{:S(2)}, u32[]{:S(2)}) %all-to-all-start.1) | async-done | bytes 1474592 | tf_op jit(solution)/shard_map/all_to_all | solution.py:22
  1227.4 71.7 %all-to-all-done = bf16[8,96,2116]{2,1,0:T(8,128)(2,1)S(1)} async-done(((bf16[8,96,2116]{2,1,0:T(8,128)(2,1)}), bf16[8,96,2116]{2,1,0:T(8,128)(2,1)S(1)}, u32[]{:S(2)}, u32[]{:S(2)}) %all-to-all-start) | async-done | bytes 3250208 | tf_op jit(solution)/shard_map/all_to_all | solution.py:22
  (611 shorter events, 398.2 us)
Async XLA Ops:
  25.1 73.9 %copy-start.9 = (bf16[96,3,192]{2,1,0:T(4,128)(2,1)}, bf16[96,3,192]{2,1,0:T(4,128)(2,1)S(1)}, u32[]{:S(2)}) copy-start(bf16[96,3,192]{2,1,0:T(4,128)(2,1)S(1)} %get-tuple-element.1742) | copy-start | bytes 331780 | tf_op jit(solution)/shard_map/while
  25.1 73.9 %copy-start.25 = (bf16[192,96]{0,1:T(8,128)(2,1)}, bf16[192,96]{0,1:T(8,128)(2,1)S(1)}, u32[]{:S(2)}) copy-start(bf16[192,96]{0,1:T(8,128)(2,1)S(1)} %get-tuple-element.1745) | copy-start | bytes 110596 | tf_op jit(solution)/shard_map/while
  25.1 74.0 %all-gather.24.cloned.1.call-start = ((), (), s32[]{:S(2)}) async-start(), calls=%async_computation.7 | async-start | bytes 1966080 | tf_op jit(solution)/shard_map/while/body/eval_jaxpr/all_gather | solution.py:88
  26.0 125.4 %reduce-scatter.5.cloned.1.call-start = ((), (), s32[]{:S(2)}) async-start(), calls=%async_computation.8 | async-start | bytes 1966080 | tf_op jit(solution)/shard_map/while/body/eval_jaxpr/reduce_scatter | solution.py:94
  114.9 81.1 %all-gather.28.cloned.1.call-start = ((), (), s32[]{:S(2)}) async-start(), calls=%async_computation.10 | async-start | bytes 2654208 | tf_op jit(solution)/shard_map/while/body/eval_jaxpr/all_gather | solution.py:107
  115.6 100.7 %all-gather.26.cloned.1.call-start = ((), (), s32[]{:S(2)}) async-start(), calls=%async_computation.9 | async-start | bytes 1966080 | tf_op jit(solution)/shard_map/while/body/eval_jaxpr/all_gather | solution.py:88
  156.4 103.0 %all-gather.22.cloned.1.call-start = ((), (), s32[]{:S(2)}) async-start(), calls=%async_computation.6 | async-start | bytes 1327104 | tf_op jit(solution)/shard_map/while/body/eval_jaxpr/all_gather | solution.py:113
  157.0 135.8 %reduce-scatter.7.cloned.1.call-start = ((), (), s32[]{:S(2)}) async-start(), calls=%async_computation.11 | async-start | bytes 1966080 | tf_op jit(solution)/shard_map/while/body/eval_jaxpr/reduce_scatter | solution.py:94
  296.8 73.4 %all-gather.24.cloned.1.call-start = ((), (), s32[]{:S(2)}) async-start(), calls=%async_computation.7 | async-start | bytes 1966080 | tf_op jit(solution)/shard_map/while/body/eval_jaxpr/all_gather | solution.py:88
  297.7 124.6 %reduce-scatter.5.cloned.1.call-start = ((), (), s32[]{:S(2)}) async-start(), calls=%async_computation.8 | async-start | bytes 1966080 | tf_op jit(solution)/shard_map/while/body/eval_jaxpr/reduce_scatter | solution.py:94
  386.0 80.6 %all-gather.28.cloned.1.call-start = ((), (), s32[]{:S(2)}) async-start(), calls=%async_computation.10 | async-start | bytes 2654208 | tf_op jit(solution)/shard_map/while/body/eval_jaxpr/all_gather | solution.py:107
  386.7 100.2 %all-gather.26.cloned.1.call-start = ((), (), s32[]{:S(2)}) async-start(), calls=%async_computation.9 | async-start | bytes 1966080 | tf_op jit(solution)/shard_map/while/body/eval_jaxpr/all_gather | solution.py:88
  427.3 102.9 %all-gather.22.cloned.1.call-start = ((), (), s32[]{:S(2)}) async-start(), calls=%async_computation.6 | async-start | bytes 1327104 | tf_op jit(solution)/shard_map/while/body/eval_jaxpr/all_gather | solution.py:113
  428.0 135.6 %reduce-scatter.7.cloned.1.call-start = ((), (), s32[]{:S(2)}) async-start(), calls=%async_computation.11 | async-start | bytes 1966080 | tf_op jit(solution)/shard_map/while/body/eval_jaxpr/reduce_scatter | solution.py:94
  588.7 155.6 %copy-start.11 = (bf16[96,3,192]{2,1,0:T(4,128)(2,1)}, bf16[96,3,192]{2,1,0:T(4,128)(2,1)S(1)}, u32[]{:S(2)}) copy-start(bf16[96,3,192]{2,1,0:T(4,128)(2,1)S(1)} %get-tuple-element.1842) | copy-start | bytes 331780 | tf_op jit(solution)/shard_map/while
  588.7 195.8 %copy-start.27 = (bf16[192,96]{0,1:T(8,128)(2,1)}, bf16[192,96]{0,1:T(8,128)(2,1)S(1)}, u32[]{:S(2)}) copy-start(bf16[192,96]{0,1:T(8,128)(2,1)S(1)} %get-tuple-element.1837) | copy-start | bytes 110596 | tf_op jit(solution)/shard_map/while
  588.7 44.1 %all-gather.34.cloned.1.call-start = ((), (), s32[]{:S(2)}) async-start(), calls=%async_computation.14 | async-start | bytes 1327104 | tf_op jit(solution)/shard_map/while/body/eval_jaxpr/all_gather | solution.py:113
  589.4 63.2 %all-gather.32.cloned.1.call-start = ((), (), s32[]{:S(2)}) async-start(), calls=%async_computation.13 | async-start | bytes 1966080 | tf_op jit(solution)/shard_map/while/body/eval_jaxpr/all_gather | solution.py:88
  614.8 92.0 %all-gather.30.cloned.1.call-start = ((), (), s32[]{:S(2)}) async-start(), calls=%async_computation.12 | async-start | bytes 2654208 | tf_op jit(solution)/shard_map/while/body/eval_jaxpr/all_gather | solution.py:107
  615.4 124.7 %reduce-scatter.9.cloned.1.call-start = ((), (), s32[]{:S(2)}) async-start(), calls=%async_computation.15 | async-start | bytes 1966080 | tf_op jit(solution)/shard_map/while/body/eval_jaxpr/reduce_scatter | solution.py:94
  713.2 112.7 %all-gather.36.cloned.1.call-start = ((), (), s32[]{:S(2)}) async-start(), calls=%async_computation.16 | async-start | bytes 1966080 | tf_op jit(solution)/shard_map/while/body/eval_jaxpr/all_gather | solution.py:88
  744.2 133.8 %reduce-scatter.11.cloned.1.call-start = ((), (), s32[]{:S(2)}) async-start(), calls=%async_computation.17 | async-start | bytes 1966080 | tf_op jit(solution)/shard_map/while/body/eval_jaxpr/reduce_scatter | solution.py:94
  880.0 155.7 %copy-start.11 = (bf16[96,3,192]{2,1,0:T(4,128)(2,1)}, bf16[96,3,192]{2,1,0:T(4,128)(2,1)S(1)}, u32[]{:S(2)}) copy-start(bf16[96,3,192]{2,1,0:T(4,128)(2,1)S(1)} %get-tuple-element.1842) | copy-start | bytes 331780 | tf_op jit(solution)/shard_map/while
  880.0 195.6 %copy-start.27 = (bf16[192,96]{0,1:T(8,128)(2,1)}, bf16[192,96]{0,1:T(8,128)(2,1)S(1)}, u32[]{:S(2)}) copy-start(bf16[192,96]{0,1:T(8,128)(2,1)S(1)} %get-tuple-element.1837) | copy-start | bytes 110596 | tf_op jit(solution)/shard_map/while
  880.0 44.1 %all-gather.34.cloned.1.call-start = ((), (), s32[]{:S(2)}) async-start(), calls=%async_computation.14 | async-start | bytes 1327104 | tf_op jit(solution)/shard_map/while/body/eval_jaxpr/all_gather | solution.py:113
  880.7 63.3 %all-gather.32.cloned.1.call-start = ((), (), s32[]{:S(2)}) async-start(), calls=%async_computation.13 | async-start | bytes 1966080 | tf_op jit(solution)/shard_map/while/body/eval_jaxpr/all_gather | solution.py:88
  906.1 92.1 %all-gather.30.cloned.1.call-start = ((), (), s32[]{:S(2)}) async-start(), calls=%async_computation.12 | async-start | bytes 2654208 | tf_op jit(solution)/shard_map/while/body/eval_jaxpr/all_gather | solution.py:107
  906.9 124.7 %reduce-scatter.9.cloned.1.call-start = ((), (), s32[]{:S(2)}) async-start(), calls=%async_computation.15 | async-start | bytes 1966080 | tf_op jit(solution)/shard_map/while/body/eval_jaxpr/reduce_scatter | solution.py:94
  1004.7 112.6 %all-gather.36.cloned.1.call-start = ((), (), s32[]{:S(2)}) async-start(), calls=%async_computation.16 | async-start | bytes 1966080 | tf_op jit(solution)/shard_map/while/body/eval_jaxpr/all_gather | solution.py:88
  1035.6 134.9 %reduce-scatter.11.cloned.1.call-start = ((), (), s32[]{:S(2)}) async-start(), calls=%async_computation.17 | async-start | bytes 1966080 | tf_op jit(solution)/shard_map/while/body/eval_jaxpr/reduce_scatter | solution.py:94
  1177.7 42.6 %all-to-all-start.1 = ((bf16[8,960,96]{1,2,0:T(8,128)(2,1)}), bf16[8,960,96]{1,2,0:T(8,128)(2,1)}, u32[]{:S(2)}, u32[]{:S(2)}) async-start(bf16[8,960,96]{1,2,0:T(8,128)(2,1)} %bitcast.41), calls=%async_computation.5 | async-start | bytes 3145728 | tf_op jit(solution)/shard_map/all_to_all | solution.py:22
  1220.3 78.7 %all-to-all-start = ((bf16[8,96,2116]{2,1,0:T(8,128)(2,1)}), bf16[8,96,2116]{2,1,0:T(8,128)(2,1)S(1)}, u32[]{:S(2)}, u32[]{:S(2)}) async-start(bf16[8,96,2116]{2,1,0:T(8,128)(2,1)} %concatenate.100), calls=%async_computation.4 | async-start | bytes 6684672 | tf_op jit(solution)/shard_map/all_to_all | solution.py:22
  (139 other events, 1216.5 us)
Sparse Core Ops, SparseCore 0:
  27.5 20.1 all-gather.23
  115.0 26.4 reduce-scatter.4
  143.9 52.0 all-gather.27
  198.1 18.1 all-gather.25
  218.3 41.0 all-gather.21
  265.9 26.9 reduce-scatter.6
  299.2 19.6 all-gather.23
  386.1 25.9 reduce-scatter.4
  414.5 52.0 all-gather.27
  468.6 18.1 all-gather.25
  489.1 41.0 all-gather.21
  536.6 26.9 reduce-scatter.6
  591.7 41.0 all-gather.33
  634.2 18.4 all-gather.31
  654.7 52.0 all-gather.29
  713.4 26.7 reduce-scatter.8
  744.3 19.6 all-gather.35
  851.6 26.3 reduce-scatter.10
  883.0 41.0 all-gather.33
  925.5 18.4 all-gather.31
  946.2 52.0 all-gather.29
  1004.8 26.6 reduce-scatter.8
  1035.7 19.6 all-gather.35
  1142.9 27.5 reduce-scatter.10
where the time goes:
time: 1340 us; the launch traced here: 1320 us
  waiting for transfers between devices  535 us (40%)
  blocking collectives  409 us (31%)
  matrix products  162 us (12%)
  local copies, waits for them, and re-layouts  95.7 us (7%)
  other arithmetic  73 us (5%)
  loops' own time  22.6 us (2%)
  between operations  14.7 us (1%)
    all_gather x4, waiting for transfers between devices, fetch_weights(): lax.all_gather(w_gate_up, 'row', axis=0, tiled=True)  170 us
    all_gather x4, blocking collectives, fetch_weights(): lax.all_gather(w_qkv, 'row', axis=0, tiled=True)  149 us
    all_gather x4, blocking collectives, fetch_weights(): lax.all_gather(w_out, 'row', axis=1, tiled=True)  124 us
    reduce_scatter x8, waiting for transfers between devices, token_sums(): lax.psum_scatter(lax.dot_general(piece, right, (((1,), (contract,)), ((),...  104 us
    all_to_all x2, waiting for transfers between devices, summed_on_arrival(): lax.all_to_all(blocks, axis, split_axis=0, concat_axis=0, tiled=True)  97.5 us
    all_gather x4, waiting for transfers between devices, fetch_weights(): lax.all_gather(w_down, 'row', axis=1, tiled=True)  80.7 us
    all_gather x4, blocking collectives, fetch_weights(): lax.all_gather(norm_gain, 'row', axis=0, tiled=True)  77.9 us
    all_gather x8, waiting for transfers between devices, gather_tokens(): return lax.all_gather(values, 'col', axis=0, tiled=True)  76.2 us
  transfers between devices with their start and end apart: 26, of which 20 were waited for; matrix products, arithmetic and copies ran while one was open for 14% of the time, Pallas kernels for 0%

commit v1 on v0

--- a/solution.py
+++ b/solution.py
@@ -9,6 +9,18 @@
 epsilon = 1e-12
 rope_base = 1000.0
 masked_score = -1e30
+
+
+def collect(value, axis, dim):
+    ways, here = (lax.axis_size(axis), lax.axis_index(axis))
+    grown, reach = (value, 1)
+    while reach < ways:
+        theirs = lax.ppermute(grown, axis, [(d, d ^ reach) for d in range(ways)])
+        mine_first = jnp.concatenate([grown, theirs], axis=dim)
+        theirs_first = jnp.concatenate([theirs, grown], axis=dim)
+        grown = jnp.where(here & reach == 0, mine_first, theirs_first)
+        reach = 2 * reach
+    return grown
 
 
 def in_blocks(array, dim, peers):
@@ -85,7 +97,7 @@
 
 
 def gather_tokens(values):
-    return lax.all_gather(values, "col", axis=0, tiled=True)
+    return collect(values, "col", 0)
 
 
 def token_sums(left, right, contract):

time: 1340 us -> 1240 us (0.925)
  waiting for transfers between devices: 535 us -> 399 us
  other arithmetic: 73 us -> 93.4 us
    all_gather x8 -> x0, waiting for transfers between devices: 76.2 us -> none  [gather_tokens(): return lax.all_gather(values, 'col', axis=0, tiled=True)]
    reduce_scatter x8, waiting for transfers between devices: 104 us -> 38.2 us  [token_sums(): lax.psum_scatter(lax.dot_general(piece, right, (((1,), (contract,)), ((),...]
    ppermute x0 -> x16, waiting for transfers between devices: none -> 38.6 us  [collect(): theirs = lax.ppermute(grown, axis, [(d, d ^ reach) for d in range(ways)])]
    all_gather x4, waiting for transfers between devices: 80.7 us -> 64.3 us  [fetch_weights(): lax.all_gather(w_down, 'row', axis=1, tiled=True)]
    all_gather x4, waiting for transfers between devices: 170 us -> 156 us  [fetch_weights(): lax.all_gather(w_gate_up, 'row', axis=0, tiled=True)]
  transfers between devices with their start and end apart: 26 -> 34, of which waited for: 20 -> 20; matrix products, arithmetic and copies ran while one was open for 14% -> 16% of each run, Pallas kernels for 0% -> 0%
where the time goes in v1:
time: 1240 us; the launch traced here: 1220 us
  blocking collectives  414 us (33%)
  waiting for transfers between devices  399 us (32%)
  matrix products  170 us (14%)
  other arithmetic  93.4 us (8%)
  local copies, waits for them, and re-layouts  87.5 us (7%)
  loops' own time  26.9 us (2%)
  starting transfers between devices  19.3 us (2%)
  between operations  14.2 us (1%)
    all_gather x4, waiting for transfers between devices, fetch_weights(): lax.all_gather(w_gate_up, 'row', axis=0, tiled=True)  156 us
    all_gather x4, blocking collectives, fetch_weights(): lax.all_gather(w_qkv, 'row', axis=0, tiled=True)  149 us
    all_gather x4, blocking collectives, fetch_weights(): lax.all_gather(w_out, 'row', axis=1, tiled=True)  129 us
    all_to_all x2, waiting for transfers between devices, summed_on_arrival(): lax.all_to_all(blocks, axis, split_axis=0, concat_axis=0, tiled=True)  97.5 us
    all_gather x4, blocking collectives, fetch_weights(): lax.all_gather(norm_gain, 'row', axis=0, tiled=True)  78.2 us
    all_gather x4, waiting for transfers between devices, fetch_weights(): lax.all_gather(w_down, 'row', axis=1, tiled=True)  64.3 us
    ppermute x16, waiting for transfers between devices, collect(): theirs = lax.ppermute(grown, axis, [(d, d ^ reach) for d in range(ways)])  38.6 us
    reduce_scatter x8, waiting for transfers between devices, token_sums(): lax.psum_scatter(lax.dot_general(piece, right, (((1,), (contract,)), ((),...  38.2 us
  transfers between devices with their start and end apart: 34, of which 20 were waited for; matrix products, arithmetic and copies ran while one was open for 16% of the time, Pallas kernels for 0%

profile of v1, /device:TPU:0, one launch (start us, length us, event | category | flops | bytes accessed | tf_op | source)
XLA Modules:
  0.0 1224.1 jit_solution(17027895789283126235)
XLA Ops:
  26.5 508.4 %while.68 = (s32[]{:T(128)}, bf16[2,256,768]{2,1,0:T(8,128)(2,1)}, bf16[2,1024,768]{2,1,0:T(8,128)(2,1)}, bf16[2,1024,3,64]{1,3,2,0:T(8,128)(2,1)}, bf16[2,1024,...) while((s32[]{:T(128)}, bf16[2,256,768]{2,1,0:T(8,128)(2,1)}, ...), condition=%wide.region_11.12_spmd, body=%wide.region_0.11_spmd.sunk | while | flops 5732602368 | bytes 167994992 | solution.py:268
  27.5 37.9 %all_gather.75 = bf16[768,3,192]{2,1,0:T(4,128)(2,1)S(1)} all-gather(bf16[96,3,192]{2,1,0:T(4,128)(2,1)} %get-tuple-element.1746), channel_id=1, replica_groups=mesh['row'=8,'col'=4] {'row'}, dimensions={0}, use_global_device_ids=true | all-gather | bytes 995328 | tf_op jit(solution)/shard_map/while/body/eval_jaxpr/all_gather | solution.py:118
  71.2 31.2 %all_gather.76 = bf16[192,768]{0,1:T(8,128)(2,1)S(1)} all-gather(bf16[192,96]{0,1:T(8,128)(2,1)} %get-tuple-element.1749), channel_id=1, replica_groups=mesh['row'=8,'col'=4] {'row'}, dimensions={1}, use_global_device_ids=true | all-gather | bytes 331776 | tf_op jit(solution)/shard_map/while/body/eval_jaxpr/all_gather | solution.py:124
  122.0 18.6 %all-gather.8 = bf16[8,96,2]{1,2,0:T(2,128)(2,1)S(1)} all-gather(bf16[1,96,2]{1,2,0:T(2,128)(2,1)S(1)} %bitcast.456), channel_id=1, replica_groups=mesh['row'=8,'col'=4] {'row'}, dimensions={0}, use_global_device_ids=true | all-gather | bytes 3456 | tf_op jit(solution)/shard_map/while/body/eval_jaxpr/all_gather | solution.py:120
  140.7 16.2 %all-gather.7 = bf16[8,96,2]{1,2,0:T(2,128)(2,1)S(1)} all-gather(bf16[1,96,2]{1,2,0:T(2,128)(2,1)S(1)} %bitcast.458), channel_id=1, replica_groups=mesh['row'=8,'col'=4] {'row'}, dimensions={0}, use_global_device_ids=true | all-gather | bytes 3456 | tf_op jit(solution)/shard_map/while/body/eval_jaxpr/all_gather | solution.py:121
  164.8 37.2 %all-gather.17.cloned.1.call-done = bf16[768,2,768]{2,1,0:T(2,128)(2,1)} async-done(((bf16[96,2,768]{2,1,0:T(2,128)(2,1)}), bf16[768,2,768]{2,1,0:T(2,128)(2,1)}) %all-gather.17.cloned.1.call-update) | async-done | bytes 2359312 | tf_op jit(solution)/shard_map/while/body/eval_jaxpr/all_gather | solution.py:119
  211.7 32.1 %all-gather.15.cloned.1.call-done = bf16[768,768]{0,1:T(8,128)(2,1)} async-done(((bf16[768,96]{0,1:T(8,128)(2,1)}), bf16[768,768]{0,1:T(8,128)(2,1)}) %all-gather.15.cloned.1.call-update) | async-done | bytes 1179664 | tf_op jit(solution)/shard_map/while/body/eval_jaxpr/all_gather | solution.py:125
  263.2 14.0 %reduce-scatter.7.cloned.1.call-done = bf16[256,768]{1,0:T(8,128)(2,1)} async-done(((bf16[1024,768]{1,0:T(8,128)(2,1)}), bf16[256,768]{1,0:T(8,128)(2,1)}) %reduce-scatter.7.cloned.1.call-update) | async-done | bytes 393232 | tf_op jit(solution)/shard_map/while/body/eval_jaxpr/reduce_scatter | solution.py:106
  281.7 37.8 %all_gather.75 = bf16[768,3,192]{2,1,0:T(4,128)(2,1)S(1)} all-gather(bf16[96,3,192]{2,1,0:T(4,128)(2,1)} %get-tuple-element.1746), channel_id=1, replica_groups=mesh['row'=8,'col'=4] {'row'}, dimensions={0}, use_global_device_ids=true | all-gather | bytes 995328 | tf_op jit(solution)/shard_map/while/body/eval_jaxpr/all_gather | solution.py:118
  325.0 31.4 %all_gather.76 = bf16[192,768]{0,1:T(8,128)(2,1)S(1)} all-gather(bf16[192,96]{0,1:T(8,128)(2,1)} %get-tuple-element.1749), channel_id=1, replica_groups=mesh['row'=8,'col'=4] {'row'}, dimensions={1}, use_global_device_ids=true | all-gather | bytes 331776 | tf_op jit(solution)/shard_map/while/body/eval_jaxpr/all_gather | solution.py:124
  375.9 18.5 %all-gather.8 = bf16[8,96,2]{1,2,0:T(2,128)(2,1)S(1)} all-gather(bf16[1,96,2]{1,2,0:T(2,128)(2,1)S(1)} %bitcast.456), channel_id=1, replica_groups=mesh['row'=8,'col'=4] {'row'}, dimensions={0}, use_global_device_ids=true | all-gather | bytes 3456 | tf_op jit(solution)/shard_map/while/body/eval_jaxpr/all_gather | solution.py:120
  394.5 16.2 %all-gather.7 = bf16[8,96,2]{1,2,0:T(2,128)(2,1)S(1)} all-gather(bf16[1,96,2]{1,2,0:T(2,128)(2,1)S(1)} %bitcast.458), channel_id=1, replica_groups=mesh['row'=8,'col'=4] {'row'}, dimensions={0}, use_global_device_ids=true | all-gather | bytes 3456 | tf_op jit(solution)/shard_map/while/body/eval_jaxpr/all_gather | solution.py:121
  418.8 37.2 %all-gather.17.cloned.1.call-done = bf16[768,2,768]{2,1,0:T(2,128)(2,1)} async-done(((bf16[96,2,768]{2,1,0:T(2,128)(2,1)}), bf16[768,2,768]{2,1,0:T(2,128)(2,1)}) %all-gather.17.cloned.1.call-update) | async-done | bytes 2359312 | tf_op jit(solution)/shard_map/while/body/eval_jaxpr/all_gather | solution.py:119
  465.6 32.2 %all-gather.15.cloned.1.call-done = bf16[768,768]{0,1:T(8,128)(2,1)} async-done(((bf16[768,96]{0,1:T(8,128)(2,1)}), bf16[768,768]{0,1:T(8,128)(2,1)}) %all-gather.15.cloned.1.call-update) | async-done | bytes 1179664 | tf_op jit(solution)/shard_map/while/body/eval_jaxpr/all_gather | solution.py:125
  517.2 13.9 %reduce-scatter.7.cloned.1.call-done = bf16[256,768]{1,0:T(8,128)(2,1)} async-done(((bf16[1024,768]{1,0:T(8,128)(2,1)}), bf16[256,768]{1,0:T(8,128)(2,1)}) %reduce-scatter.7.cloned.1.call-update) | async-done | bytes 393232 | tf_op jit(solution)/shard_map/while/body/eval_jaxpr/reduce_scatter | solution.py:106
  536.1 539.1 %while.69 = (s32[]{:T(128)}, f32[768,576]{0,1:T(8,128)}, f32[192,768]{1,0:T(8,128)}, f32[768,1536]{1,0:T(8,128)}, f32[768,768]{1,0:T(8,128)}, /*index=5*/f32[768...) while((s32[]{:T(128)}, f32[768,576]{0,1:T(8,128)}, ...), condition=%wide.region_25.26_spmd.clone, body=%wide.region_12.25_spmd.clone.sunk | while | flops 11806512128 | bytes 363707328 | solution.py:356
  558.4 20.5 %all-gather.9 = bf16[8,96,2]{1,2,0:T(2,128)(2,1)S(1)} all-gather(bf16[1,96,2]{1,2,0:T(2,128)(2,1)} %bitcast.457), channel_id=1, replica_groups=mesh['row'=8,'col'=4] {'row'}, dimensions={0}, use_global_device_ids=true | all-gather | bytes 3456 | tf_op jit(solution)/shard_map/while/body/eval_jaxpr/all_gather | solution.py:120
  605.3 7.9 multiply_convert_fusion.13
  613.2 40.6 %all-gather.19.cloned.1.call-done = bf16[768,2,768]{2,1,0:T(2,128)(2,1)} async-done(((bf16[96,2,768]{2,1,0:T(2,128)(2,1)}), bf16[768,2,768]{2,1,0:T(2,128)(2,1)}) %all-gather.19.cloned.1.call-update) | async-done | bytes 2359312 | tf_op jit(solution)/shard_map/while/body/eval_jaxpr/all_gather | solution.py:119
  661.0 33.2 %all_gather.77 = bf16[192,768]{0,1:T(8,128)(2,1)} all-gather(bf16[192,96]{0,1:T(8,128)(2,1)S(1)} %copy-done.14), channel_id=1, replica_groups=mesh['row'=8,'col'=4] {'row'}, dimensions={1}, use_global_device_ids=true | all-gather | bytes 331776 | tf_op jit(solution)/shard_map/while/body/eval_jaxpr/all_gather | solution.py:124
  703.9 37.0 %all_gather.80 = bf16[768,3,192]{2,1,0:T(4,128)(2,1)S(1)} all-gather(bf16[96,3,192]{2,1,0:T(4,128)(2,1)} %get-tuple-element.1852), channel_id=1, replica_groups=mesh['row'=8,'col'=4] {'row'}, dimensions={0}, use_global_device_ids=true | all-gather | bytes 995328 | tf_op jit(solution)/shard_map/while/body/eval_jaxpr/all_gather | solution.py:118
  750.0 9.4 collective-permute-done.7
  815.5 20.6 %all-gather.9 = bf16[8,96,2]{1,2,0:T(2,128)(2,1)S(1)} all-gather(bf16[1,96,2]{1,2,0:T(2,128)(2,1)} %bitcast.457), channel_id=1, replica_groups=mesh['row'=8,'col'=4] {'row'}, dimensions={0}, use_global_device_ids=true | all-gather | bytes 3456 | tf_op jit(solution)/shard_map/while/body/eval_jaxpr/all_gather | solution.py:120
  870.5 40.6 %all-gather.19.cloned.1.call-done = bf16[768,2,768]{2,1,0:T(2,128)(2,1)} async-done(((bf16[96,2,768]{2,1,0:T(2,128)(2,1)}), bf16[768,2,768]{2,1,0:T(2,128)(2,1)}) %all-gather.19.cloned.1.call-update) | async-done | bytes 2359312 | tf_op jit(solution)/shard_map/while/body/eval_jaxpr/all_gather | solution.py:119
  918.3 33.2 %all_gather.77 = bf16[192,768]{0,1:T(8,128)(2,1)} all-gather(bf16[192,96]{0,1:T(8,128)(2,1)S(1)} %copy-done.14), channel_id=1, replica_groups=mesh['row'=8,'col'=4] {'row'}, dimensions={1}, use_global_device_ids=true | all-gather | bytes 331776 | tf_op jit(solution)/shard_map/while/body/eval_jaxpr/all_gather | solution.py:124
  961.2 36.6 %all_gather.80 = bf16[768,3,192]{2,1,0:T(4,128)(2,1)S(1)} all-gather(bf16[96,3,192]{2,1,0:T(4,128)(2,1)} %get-tuple-element.1852), channel_id=1, replica_groups=mesh['row'=8,'col'=4] {'row'}, dimensions={0}, use_global_device_ids=true | all-gather | bytes 995328 | tf_op jit(solution)/shard_map/while/body/eval_jaxpr/all_gather | solution.py:118
  1007.7 9.0 collective-permute-done.7
  1041.9 8.0 select_add_fusion.8
  1049.9 7.9 select_add_fusion.7
  1097.1 25.8 %all-to-all-done.1 = bf16[8,960,96]{1,2,0:T(8,128)(2,1)} async-done(((bf16[8,960,96]{1,2,0:T(8,128)(2,1)}), bf16[8,960,96]{1,2,0:T(8,128)(2,1)}, u32[]{:S(2)}, u32[]{:S(2)}) %all-to-all-start.1) | async-done | bytes 1474592 | tf_op jit(solution)/shard_map/all_to_all | solution.py:34
  1129.9 71.7 %all-to-all-done = bf16[8,96,2116]{2,1,0:T(8,128)(2,1)S(1)} async-done(((bf16[8,96,2116]{2,1,0:T(8,128)(2,1)}), bf16[8,96,2116]{2,1,0:T(8,128)(2,1)S(1)}, u32[]{:S(2)}, u32[]{:S(2)}) %all-to-all-start) | async-done | bytes 3250208 | tf_op jit(solution)/shard_map/all_to_all | solution.py:34
  1202.4 11.5 all-reduce
  (599 shorter events, 395.1 us)
Async XLA Ops:
  26.5 131.2 %reduce-scatter.5.cloned.1.call-start = ((), (), s32[]{:S(2)}) async-start(), calls=%async_computation.8 | async-start | bytes 1966080 | tf_op jit(solution)/shard_map/while/body/eval_jaxpr/reduce_scatter | solution.py:106
  26.5 38.9 %collective-permute-start = (bf16[256,768]{1,0:T(8,128)(2,1)S(1)}, bf16[256,768]{1,0:T(8,128)(2,1)}, u32[]{:S(2)}, u32[]{:S(2)}) collective-permute-start(bf16[256,768]{1,0:T(8,128)(2,1)S(1)} %dynamic-slice_bitcast_fusion.14), channel_id=1, source_target_pairs={{0,1},{1,0},{2,3},{3,2},{4,5},{5,4},{6,7},{7,6},{8,9},{9,8},{10,11... | collective-permute-start | bytes 1179656 | tf_op jit(solution)/shard_map/while/body/eval_jaxpr/ppermute | solution.py:18
  67.6 36.6 %collective-permute-start.1 = (bf16[512,768]{1,0:T(8,128)(2,1)}, bf16[512,768]{1,0:T(8,128)(2,1)}, u32[]{:S(2)}, u32[]{:S(2)}) collective-permute-start(bf16[512,768]{1,0:T(8,128)(2,1)} %maximum_select_fusion.22), channel_id=1, source_target_pairs={{0,2},{1,3},{2,0},{3,1},{4,6},{5,7},{6,4},{7,5},{8,10},{9,11},{10,... | collective-permute-start | bytes 2359304 | tf_op jit(solution)/shard_map/while/body/eval_jaxpr/ppermute | solution.py:18
  120.5 81.5 %all-gather.17.cloned.1.call-start = ((), (), s32[]{:S(2)}) async-start(), calls=%async_computation.7 | async-start | bytes 2654208 | tf_op jit(solution)/shard_map/while/body/eval_jaxpr/all_gather | solution.py:119
  121.2 122.6 %all-gather.15.cloned.1.call-start = ((), (), s32[]{:S(2)}) async-start(), calls=%async_computation.6 | async-start | bytes 1327104 | tf_op jit(solution)/shard_map/while/body/eval_jaxpr/all_gather | solution.py:125
  122.0 155.1 %reduce-scatter.7.cloned.1.call-start = ((), (), s32[]{:S(2)}) async-start(), calls=%async_computation.9 | async-start | bytes 1966080 | tf_op jit(solution)/shard_map/while/body/eval_jaxpr/reduce_scatter | solution.py:106
  161.3 1.8 collective-permute-start.2
  163.4 40.6 %collective-permute-start.3 = (bf16[512,768]{1,0:T(8,128)(2,1)S(1)}, bf16[512,768]{1,0:T(8,128)(2,1)}, u32[]{:S(2)}, u32[]{:S(2)}) collective-permute-start(bf16[512,768]{1,0:T(8,128)(2,1)S(1)} %maximum_select_fusion.23), channel_id=1, source_target_pairs={{0,2},{1,3},{2,0},{3,1},{4,6},{5,7},{6,4},{7,5},{8,10},{9,11},{10,... | collective-permute-start | bytes 2359304 | tf_op jit(solution)/shard_map/while/body/eval_jaxpr/ppermute | solution.py:18
  280.9 130.5 %reduce-scatter.5.cloned.1.call-start = ((), (), s32[]{:S(2)}) async-start(), calls=%async_computation.8 | async-start | bytes 1966080 | tf_op jit(solution)/shard_map/while/body/eval_jaxpr/reduce_scatter | solution.py:106
  280.9 38.5 %collective-permute-start = (bf16[256,768]{1,0:T(8,128)(2,1)S(1)}, bf16[256,768]{1,0:T(8,128)(2,1)}, u32[]{:S(2)}, u32[]{:S(2)}) collective-permute-start(bf16[256,768]{1,0:T(8,128)(2,1)S(1)} %dynamic-slice_bitcast_fusion.14), channel_id=1, source_target_pairs={{0,1},{1,0},{2,3},{3,2},{4,5},{5,4},{6,7},{7,6},{8,9},{9,8},{10,11... | collective-permute-start | bytes 1179656 | tf_op jit(solution)/shard_map/while/body/eval_jaxpr/ppermute | solution.py:18
  321.7 36.6 %collective-permute-start.1 = (bf16[512,768]{1,0:T(8,128)(2,1)}, bf16[512,768]{1,0:T(8,128)(2,1)}, u32[]{:S(2)}, u32[]{:S(2)}) collective-permute-start(bf16[512,768]{1,0:T(8,128)(2,1)} %maximum_select_fusion.22), channel_id=1, source_target_pairs={{0,2},{1,3},{2,0},{3,1},{4,6},{5,7},{6,4},{7,5},{8,10},{9,11},{10,... | collective-permute-start | bytes 2359304 | tf_op jit(solution)/shard_map/while/body/eval_jaxpr/ppermute | solution.py:18
  374.5 81.5 %all-gather.17.cloned.1.call-start = ((), (), s32[]{:S(2)}) async-start(), calls=%async_computation.7 | async-start | bytes 2654208 | tf_op jit(solution)/shard_map/while/body/eval_jaxpr/all_gather | solution.py:119
  375.1 122.7 %all-gather.15.cloned.1.call-start = ((), (), s32[]{:S(2)}) async-start(), calls=%async_computation.6 | async-start | bytes 1327104 | tf_op jit(solution)/shard_map/while/body/eval_jaxpr/all_gather | solution.py:125
  375.8 155.3 %reduce-scatter.7.cloned.1.call-start = ((), (), s32[]{:S(2)}) async-start(), calls=%async_computation.9 | async-start | bytes 1966080 | tf_op jit(solution)/shard_map/while/body/eval_jaxpr/reduce_scatter | solution.py:106
  415.1 1.8 collective-permute-start.2
  417.2 40.9 %collective-permute-start.3 = (bf16[512,768]{1,0:T(8,128)(2,1)S(1)}, bf16[512,768]{1,0:T(8,128)(2,1)}, u32[]{:S(2)}, u32[]{:S(2)}) collective-permute-start(bf16[512,768]{1,0:T(8,128)(2,1)S(1)} %maximum_select_fusion.23), channel_id=1, source_target_pairs={{0,2},{1,3},{2,0},{3,1},{4,6},{5,7},{6,4},{7,5},{8,10},{9,11},{10,... | collective-permute-start | bytes 2359304 | tf_op jit(solution)/shard_map/while/body/eval_jaxpr/ppermute | solution.py:18
  557.0 48.3 %all-gather.21.cloned.1.call-start = ((), (), s32[]{:S(2)}) async-start(), calls=%async_computation.11 | async-start | bytes 1327104 | tf_op jit(solution)/shard_map/while/body/eval_jaxpr/all_gather | solution.py:125
  557.7 96.2 %all-gather.19.cloned.1.call-start = ((), (), s32[]{:S(2)}) async-start(), calls=%async_computation.10 | async-start | bytes 2654208 | tf_op jit(solution)/shard_map/while/body/eval_jaxpr/all_gather | solution.py:119
  558.3 141.8 %reduce-scatter.9.cloned.1.call-start = ((), (), s32[]{:S(2)}) async-start(), calls=%async_computation.12 | async-start | bytes 1966080 | tf_op jit(solution)/shard_map/while/body/eval_jaxpr/reduce_scatter | solution.py:106
  585.6 19.8 %collective-permute-start.5 = (bf16[512,768]{1,0:T(8,128)(2,1)S(1)}, bf16[512,768]{1,0:T(8,128)(2,1)}, u32[]{:S(2)}, u32[]{:S(2)}) collective-permute-start(bf16[512,768]{1,0:T(8,128)(2,1)S(1)} %maximum_select_fusion.27), channel_id=1, source_target_pairs={{0,2},{1,3},{2,0},{3,1},{4,6},{5,7},{6,4},{7,5},{8,10},{9,11},{10,... | collective-permute-start | bytes 2359304 | tf_op jit(solution)/shard_map/while/body/eval_jaxpr/ppermute | solution.py:18
  660.3 151.6 %reduce-scatter.11.cloned.1.call-start = ((), (), s32[]{:S(2)}) async-start(), calls=%async_computation.13 | async-start | bytes 1966080 | tf_op jit(solution)/shard_map/while/body/eval_jaxpr/reduce_scatter | solution.py:106
  703.8 37.1 %collective-permute-start.6 = (bf16[256,768]{1,0:T(8,128)(2,1)S(1)}, bf16[256,768]{1,0:T(8,128)(2,1)}, u32[]{:S(2)}, u32[]{:S(2)}) collective-permute-start(bf16[256,768]{1,0:T(8,128)(2,1)S(1)} %get-tuple-element.1648), channel_id=1, source_target_pairs={{0,1},{1,0},{2,3},{3,2},{4,5},{5,4},{6,7},{7,6},{8,9},{9,8},{10,11... | collective-permute-start | bytes 1179656 | tf_op jit(solution)/shard_map/while/body/eval_jaxpr/ppermute | solution.py:18
  743.2 16.2 %collective-permute-start.7 = (bf16[512,768]{1,0:T(8,128)(2,1)}, bf16[512,768]{1,0:T(8,128)(2,1)}, u32[]{:S(2)}, u32[]{:S(2)}) collective-permute-start(bf16[512,768]{1,0:T(8,128)(2,1)} %maximum_select_fusion.28), channel_id=1, source_target_pairs={{0,2},{1,3},{2,0},{3,1},{4,6},{5,7},{6,4},{7,5},{8,10},{9,11},{10,... | collective-permute-start | bytes 2359304 | tf_op jit(solution)/shard_map/while/body/eval_jaxpr/ppermute | solution.py:18
  814.2 48.4 %all-gather.21.cloned.1.call-start = ((), (), s32[]{:S(2)}) async-start(), calls=%async_computation.11 | async-start | bytes 1327104 | tf_op jit(solution)/shard_map/while/body/eval_jaxpr/all_gather | solution.py:125
  814.9 96.2 %all-gather.19.cloned.1.call-start = ((), (), s32[]{:S(2)}) async-start(), calls=%async_computation.10 | async-start | bytes 2654208 | tf_op jit(solution)/shard_map/while/body/eval_jaxpr/all_gather | solution.py:119
  815.5 141.9 %reduce-scatter.9.cloned.1.call-start = ((), (), s32[]{:S(2)}) async-start(), calls=%async_computation.12 | async-start | bytes 1966080 | tf_op jit(solution)/shard_map/while/body/eval_jaxpr/reduce_scatter | solution.py:106
  842.8 19.8 %collective-permute-start.5 = (bf16[512,768]{1,0:T(8,128)(2,1)S(1)}, bf16[512,768]{1,0:T(8,128)(2,1)}, u32[]{:S(2)}, u32[]{:S(2)}) collective-permute-start(bf16[512,768]{1,0:T(8,128)(2,1)S(1)} %maximum_select_fusion.27), channel_id=1, source_target_pairs={{0,2},{1,3},{2,0},{3,1},{4,6},{5,7},{6,4},{7,5},{8,10},{9,11},{10,... | collective-permute-start | bytes 2359304 | tf_op jit(solution)/shard_map/while/body/eval_jaxpr/ppermute | solution.py:18
  917.6 151.5 %reduce-scatter.11.cloned.1.call-start = ((), (), s32[]{:S(2)}) async-start(), calls=%async_computation.13 | async-start | bytes 1966080 | tf_op jit(solution)/shard_map/while/body/eval_jaxpr/reduce_scatter | solution.py:106
  961.0 36.7 %collective-permute-start.6 = (bf16[256,768]{1,0:T(8,128)(2,1)S(1)}, bf16[256,768]{1,0:T(8,128)(2,1)}, u32[]{:S(2)}, u32[]{:S(2)}) collective-permute-start(bf16[256,768]{1,0:T(8,128)(2,1)S(1)} %get-tuple-element.1648), channel_id=1, source_target_pairs={{0,1},{1,0},{2,3},{3,2},{4,5},{5,4},{6,7},{7,6},{8,9},{9,8},{10,11... | collective-permute-start | bytes 1179656 | tf_op jit(solution)/shard_map/while/body/eval_jaxpr/ppermute | solution.py:18
  1000.0 16.7 %collective-permute-start.7 = (bf16[512,768]{1,0:T(8,128)(2,1)}, bf16[512,768]{1,0:T(8,128)(2,1)}, u32[]{:S(2)}, u32[]{:S(2)}) collective-permute-start(bf16[512,768]{1,0:T(8,128)(2,1)} %maximum_select_fusion.28), channel_id=1, source_target_pairs={{0,2},{1,3},{2,0},{3,1},{4,6},{5,7},{6,4},{7,5},{8,10},{9,11},{10,... | collective-permute-start | bytes 2359304 | tf_op jit(solution)/shard_map/while/body/eval_jaxpr/ppermute | solution.py:18
  1080.3 42.6 %all-to-all-start.1 = ((bf16[8,960,96]{1,2,0:T(8,128)(2,1)}), bf16[8,960,96]{1,2,0:T(8,128)(2,1)}, u32[]{:S(2)}, u32[]{:S(2)}) async-start(bf16[8,960,96]{1,2,0:T(8,128)(2,1)} %bitcast.43), calls=%async_computation.5 | async-start | bytes 3145728 | tf_op jit(solution)/shard_map/all_to_all | solution.py:34
  1122.9 78.7 %all-to-all-start = ((bf16[8,96,2116]{2,1,0:T(8,128)(2,1)}), bf16[8,96,2116]{2,1,0:T(8,128)(2,1)S(1)}, u32[]{:S(2)}, u32[]{:S(2)}) async-start(bf16[8,96,2116]{2,1,0:T(8,128)(2,1)} %concatenate.260), calls=%async_computation.4 | async-start | bytes 6684672 | tf_op jit(solution)/shard_map/all_to_all | solution.py:34
  (135 other events, 1098.6 us)
Sparse Core Ops, SparseCore 0:
  120.6 27.0 reduce-scatter.4
  149.9 52.0 all-gather.16
  204.2 39.5 all-gather.14
  250.1 26.9 reduce-scatter.6
  374.6 27.1 reduce-scatter.4
  403.9 52.0 all-gather.16
  458.2 39.5 all-gather.14
  504.1 26.9 reduce-scatter.6
  560.0 40.9 all-gather.20
  603.0 50.8 all-gather.18
  660.4 26.6 reduce-scatter.8
  784.5 27.3 reduce-scatter.10
  817.2 40.9 all-gather.20
  860.2 50.8 all-gather.18
  917.7 26.7 reduce-scatter.8
  1041.9 27.2 reduce-scatter.10
